TPU v7x, 32 devices: a whole 2x2x4 slice. The times are simulated.
32 devices in a mesh: dp: 8 (over z, x), fsdp: 4 (over y, core).
Axes of the slice: x: 2, y: 2, z: 4, core: 2. Of those that a mesh axis runs over, the one named last changes fastest.
Arguments:
- tokens: bfloat16 [8192, 2048], P(('dp', 'fsdp')), may hold values from -6 to 6
- segments: int32 [8192], P(('dp', 'fsdp')), may hold values from 0 to 3, as said below
- gain_attn: float32 [2048], P('dp'), may hold values from 0.1 to 1.9
- w_query: float32 [2048, 2048], P('dp', 'fsdp'), may hold values from -0.125 to 0.125
- w_key: float32 [2048, 256], P('dp', 'fsdp'), may hold values from -0.125 to 0.125
- w_value: float32 [2048, 256], P('dp', 'fsdp'), may hold values from -0.125 to 0.125
- w_out: float32 [2048, 2048], P('fsdp', 'dp'), may hold values from -0.75 to 0.75
- gain_mlp: float32 [2048], P('dp'), may hold values from 0.1 to 1.9
- w_gate: float32 [2048, 5632], P('dp', 'fsdp'), may hold values from -0.125 to 0.125
- w_up: float32 [2048, 5632], P('dp', 'fsdp'), may hold values from -0.125 to 0.125
- w_down: float32 [5632, 2048], P('fsdp', 'dp'), may hold values from -0.078125 to 0.078125
- cotangent: bfloat16 [8192, 2048], P(('dp', 'fsdp')), may hold values from -6 to 6
Outputs:
- layer_out: bfloat16 [8192, 2048], P(('dp', 'fsdp'))
- grad_tokens: bfloat16 [8192, 2048], P(('dp', 'fsdp'))
- grad_gain_attn: float32 [2048], P('dp')
- grad_w_query: float32 [2048, 2048], P('dp', 'fsdp')
- grad_w_key: float32 [2048, 256], P('dp', 'fsdp')
- grad_w_value: float32 [2048, 256], P('dp', 'fsdp')
- grad_w_out: float32 [2048, 2048], P('fsdp', 'dp')
- grad_gain_mlp: float32 [2048], P('dp')
- grad_w_gate: float32 [2048, 5632], P('dp', 'fsdp')
- grad_w_up: float32 [2048, 5632], P('dp', 'fsdp')
- grad_w_down: float32 [5632, 2048], P('fsdp', 'dp')
Inputs may be any that keep to these rules, and one draw needn't show every extreme that they name: `segments`: on each device's 256 tokens the ids number 1 to 4 whole sequences from 0 up, never falling; every sequence has 64, 128 or 256 tokens; some device holds one sequence and some four.
All inputs are finite; a program needn't handle non-finite values.
Results may differ from a plain program's by a relative error of at most 0.02.
Values may be sent and summed in bfloat16 or wider, within the bound.
No kernel may reach another device: no remote copies, remote signals or barrier semaphores. Data moves between devices by JAX's collectives and lax.ppermute only.
A program may use at most 448 MiB of HBM per device.

v0:
```python
import math
import jax
import jax.numpy as jnp
from jax import lax
from jax.sharding import PartitionSpec as P

HEAD_DIM = 64
EPSILON = 1e-05
rope_base = 10000.0


def tables(segment_block):
    rows_here = segment_block.shape[0]
    places = jnp.arange(rows_here, dtype=jnp.int32)
    same_segment = segment_block[:, None] == segment_block[None, :]
    first_index = jnp.min(jnp.where(same_segment, places[None, :], rows_here), axis=1)
    offsets = (places - first_index).astype(jnp.float32)
    half_dim = HEAD_DIM // 2
    frequencies = jnp.exp(
        jnp.arange(half_dim, dtype=jnp.float32) * (-2.0 * math.log(rope_base) / HEAD_DIM)
    )
    angles = offsets[:, None] * frequencies[None, :]
    cosine = jnp.concatenate([jnp.cos(angles), jnp.cos(angles)], axis=1)[:, None, :]
    sine_part = jnp.concatenate([jnp.sin(angles), jnp.sin(angles)], axis=1)[:, None, :]
    allowed = same_segment & (places[:, None] >= places[None, :])
    return (cosine, sine_part, allowed)


def rotate(values, cosine, sine_part):
    half_dim = values.shape[-1] // 2
    turned = jnp.concatenate([-values[..., half_dim:], values[..., :half_dim]], axis=-1)
    return values * cosine + turned * sine_part


def group_inputs(tokens, segments, cotangent):
    return (tokens, segments, cotangent, 1)


def attention_weights(gain_attn, w_query, w_key, w_value, w_out):
    low_type = jnp.bfloat16
    rows_full = (
        lax.all_gather(gain_attn.astype(low_type), "dp", axis=0, tiled=True),
        lax.all_gather(w_query.astype(low_type), "dp", axis=0, tiled=True),
        lax.all_gather(w_key.astype(low_type), "dp", axis=0, tiled=True),
        lax.all_gather(w_value.astype(low_type), "dp", axis=0, tiled=True),
        lax.all_gather(w_out.astype(low_type), "dp", axis=1, tiled=True),
    )
    wide_cols = (
        lax.all_gather(rows_full[1], "fsdp", axis=1, tiled=True),
        lax.all_gather(rows_full[2], "fsdp", axis=1, tiled=True),
        lax.all_gather(rows_full[3], "fsdp", axis=1, tiled=True),
        lax.all_gather(rows_full[4], "fsdp", axis=0, tiled=True),
    )
    return (rows_full[0], wide_cols[0], wide_cols[1], wide_cols[2], wide_cols[3])


def feed_weights(gain_mlp, w_gate, w_up, w_down):
    low_type = jnp.bfloat16
    rows_full = (
        lax.all_gather(gain_mlp.astype(low_type), "dp", axis=0, tiled=True),
        lax.all_gather(w_gate.astype(low_type), "dp", axis=0, tiled=True),
        lax.all_gather(w_up.astype(low_type), "dp", axis=0, tiled=True),
        lax.all_gather(w_down.astype(low_type), "dp", axis=1, tiled=True),
    )
    wide_cols = (
        lax.all_gather(rows_full[1], "fsdp", axis=1, tiled=True),
        lax.all_gather(rows_full[2], "fsdp", axis=1, tiled=True),
        lax.all_gather(rows_full[3], "fsdp", axis=0, tiled=True),
    )
    return (rows_full[0], wide_cols[0], wide_cols[1], wide_cols[2])


def reduce_attention(grad_gain, grad_query, grad_key, grad_value, grad_output):
    terms = (
        lax.psum_scatter(
            jnp.tile(grad_gain, lax.axis_size("fsdp")).astype(jnp.bfloat16),
            "fsdp",
            scatter_dimension=0,
            tiled=True,
        ).astype(jnp.float32),
        lax.psum_scatter(
            grad_query.astype(jnp.bfloat16), "fsdp", scatter_dimension=1, tiled=True
        ).astype(jnp.float32),
        lax.psum_scatter(
            grad_key.astype(jnp.bfloat16), "fsdp", scatter_dimension=1, tiled=True
        ).astype(jnp.float32),
        lax.psum_scatter(
            grad_value.astype(jnp.bfloat16), "fsdp", scatter_dimension=1, tiled=True
        ).astype(jnp.float32),
        lax.psum_scatter(
            grad_output.astype(jnp.bfloat16), "fsdp", scatter_dimension=0, tiled=True
        ).astype(jnp.float32),
    )
    return (
        lax.psum_scatter(
            terms[0].astype(jnp.bfloat16), "dp", scatter_dimension=0, tiled=True
        ).astype(jnp.float32),
        lax.psum_scatter(
            terms[1].astype(jnp.bfloat16), "dp", scatter_dimension=0, tiled=True
        ).astype(jnp.float32),
        lax.psum_scatter(
            terms[2].astype(jnp.bfloat16), "dp", scatter_dimension=0, tiled=True
        ).astype(jnp.float32),
        lax.psum_scatter(
            terms[3].astype(jnp.bfloat16), "dp", scatter_dimension=0, tiled=True
        ).astype(jnp.float32),
        lax.psum_scatter(
            terms[4].astype(jnp.bfloat16), "dp", scatter_dimension=1, tiled=True
        ).astype(jnp.float32),
    )


def reduce_feed(grad_gain, grad_gate, grad_upward, grad_down):
    terms = (
        lax.psum_scatter(
            jnp.tile(grad_gain, lax.axis_size("fsdp")).astype(jnp.bfloat16),
            "fsdp",
            scatter_dimension=0,
            tiled=True,
        ).astype(jnp.float32),
        lax.psum_scatter(
            grad_gate.astype(jnp.bfloat16), "fsdp", scatter_dimension=1, tiled=True
        ).astype(jnp.float32),
        lax.psum_scatter(
            grad_upward.astype(jnp.bfloat16), "fsdp", scatter_dimension=1, tiled=True
        ).astype(jnp.float32),
        lax.psum_scatter(
            grad_down.astype(jnp.bfloat16), "fsdp", scatter_dimension=0, tiled=True
        ).astype(jnp.float32),
    )
    return (
        lax.psum_scatter(
            terms[0].astype(jnp.bfloat16), "dp", scatter_dimension=0, tiled=True
        ).astype(jnp.float32),
        lax.psum_scatter(
            terms[1].astype(jnp.bfloat16), "dp", scatter_dimension=0, tiled=True
        ).astype(jnp.float32),
        lax.psum_scatter(
            terms[2].astype(jnp.bfloat16), "dp", scatter_dimension=0, tiled=True
        ).astype(jnp.float32),
        lax.psum_scatter(
            terms[3].astype(jnp.bfloat16), "dp", scatter_dimension=1, tiled=True
        ).astype(jnp.float32),
    )


def on_device(
    tokens,
    segments,
    gain_attn,
    w_query,
    w_key,
    w_value,
    w_out,
    gain_mlp,
    w_gate,
    w_up,
    w_down,
    cotangent,
):
    low_type = jnp.bfloat16
    wide_type = jnp.float32
    score_scale = HEAD_DIM ** (-0.5)
    token_rows, segment_rows, cotangent_rows, blocks = group_inputs(tokens, segments, cotangent)
    rows_all = token_rows.shape[0]
    block_rows = rows_all // blocks
    attn_full = attention_weights(gain_attn, w_query, w_key, w_value, w_out)
    feed_full = feed_weights(gain_mlp, w_gate, w_up, w_down)
    gain_one = attn_full[0].astype(wide_type)
    query_full, key_full, value_full, out_full = (
        attn_full[1],
        attn_full[2],
        attn_full[3],
        attn_full[4],
    )
    gain_two = feed_full[0].astype(wide_type)
    gate_full, up_full, down_full = (feed_full[1], feed_full[2], feed_full[3])
    heads_here = query_full.shape[1] // HEAD_DIM
    kv_here = key_full.shape[1] // HEAD_DIM
    group_size = heads_here // kv_here
    token_float = token_rows.astype(wide_type)
    inv_first = lax.rsqrt(jnp.mean(token_float * token_float, axis=-1, keepdims=True) + EPSILON)
    unit_attn = token_float * inv_first
    normed = (unit_attn * gain_one).astype(low_type)
    cosine, sine_part, allowed = jax.vmap(tables)(segment_rows.reshape(blocks, block_rows))
    query_proj = jnp.dot(normed, query_full, preferred_element_type=wide_type).reshape(
        blocks, block_rows, heads_here, HEAD_DIM
    )
    keys_proj = jnp.dot(normed, key_full, preferred_element_type=wide_type).reshape(
        blocks, block_rows, kv_here, HEAD_DIM
    )
    values_low = (
        jnp.dot(normed, value_full, preferred_element_type=wide_type)
        .astype(low_type)
        .reshape(blocks, block_rows, kv_here, HEAD_DIM)
    )
    query_rot = (
        rotate(query_proj, cosine, sine_part)
        .astype(low_type)
        .reshape(blocks, block_rows, kv_here, group_size, HEAD_DIM)
    )
    keys_rot = rotate(keys_proj, cosine, sine_part).astype(low_type)
    scores = (
        jnp.einsum("btgrd,bugd->bgrtu", query_rot, keys_rot, preferred_element_type=wide_type)
        * score_scale
    )
    masked = jnp.where(allowed[:, None, None], scores, -1e30)
    row_peak = jnp.max(masked, axis=-1, keepdims=True)
    exponent = jnp.exp(masked - row_peak)
    row_total = jnp.sum(exponent, axis=-1, keepdims=True)
    weights_soft = exponent / row_total
    log_total = row_peak + jnp.log(row_total)
    mixed_heads = jnp.einsum(
        "bgrtu,bugd->btgrd",
        weights_soft.astype(low_type),
        values_low,
        preferred_element_type=wide_type,
    )
    mixed_heads = mixed_heads.reshape(rows_all, heads_here * HEAD_DIM).astype(low_type)
    hidden = token_float + jnp.dot(mixed_heads, out_full, preferred_element_type=wide_type)
    inv_second = lax.rsqrt(jnp.mean(hidden * hidden, axis=-1, keepdims=True) + EPSILON)
    unit_mlp = hidden * inv_second
    normed_mlp = (unit_mlp * gain_two).astype(low_type)
    gate_proj = jnp.dot(normed_mlp, gate_full, preferred_element_type=wide_type)
    upward = jnp.dot(normed_mlp, up_full, preferred_element_type=wide_type)
    gate_sigmoid = jax.nn.sigmoid(gate_proj)
    activation = (gate_proj * gate_sigmoid * upward).astype(low_type)
    down_terms = jnp.dot(activation, down_full, preferred_element_type=wide_type)
    layer_out = (hidden + down_terms).astype(low_type)
    feed_back = feed_weights(gain_mlp, w_gate, w_up, w_down)
    gate_back, up_back, down_back = (feed_back[1], feed_back[2], feed_back[3])
    grad_down = jnp.einsum(
        "tf,td->fd", activation, cotangent_rows, preferred_element_type=wide_type
    )
    grad_act = jnp.einsum("td,fd->tf", cotangent_rows, down_back, preferred_element_type=wide_type)
    grad_gate = (
        grad_act * upward * gate_sigmoid * (1.0 + gate_proj * (1.0 - gate_sigmoid))
    ).astype(low_type)
    grad_upward = (grad_act * gate_proj * gate_sigmoid).astype(low_type)
    grad_w_gate = jnp.einsum("tc,tf->cf", normed_mlp, grad_gate, preferred_element_type=wide_type)
    grad_w_up = jnp.einsum("tc,tf->cf", normed_mlp, grad_upward, preferred_element_type=wide_type)
    grad_normed_mlp = jnp.einsum(
        "tf,cf->tc", grad_gate, gate_back, preferred_element_type=wide_type
    )
    grad_normed_mlp = grad_normed_mlp + jnp.einsum(
        "tf,cf->tc", grad_upward, up_back, preferred_element_type=wide_type
    )
    grad_gain_mlp = jnp.sum(grad_normed_mlp * unit_mlp, axis=0)
    scaled_mlp = grad_normed_mlp * gain_two
    grad_hidden = cotangent_rows.astype(wide_type) + inv_second * (
        scaled_mlp - unit_mlp * jnp.mean(scaled_mlp * unit_mlp, axis=-1, keepdims=True)
    )
    feed_grads = reduce_feed(grad_gain_mlp, grad_w_gate, grad_w_up, grad_down)
    attn_back = attention_weights(gain_attn, w_query, w_key, w_value, w_out)
    query_back, key_back, value_back, out_back = (
        attn_back[1],
        attn_back[2],
        attn_back[3],
        attn_back[4],
    )
    grad_branch = grad_hidden.astype(low_type)
    grad_w_out = jnp.einsum("tc,td->cd", mixed_heads, grad_branch, preferred_element_type=wide_type)
    grad_mixed = jnp.einsum(
        "td,cd->tc", grad_branch, out_back, preferred_element_type=wide_type
    ).astype(low_type)
    grad_mixed = grad_mixed.reshape(blocks, block_rows, kv_here, group_size, HEAD_DIM)
    scores_again = (
        jnp.einsum("btgrd,bugd->bgrtu", query_rot, keys_rot, preferred_element_type=wide_type)
        * score_scale
    )
    weights_again = jnp.exp(jnp.where(allowed[:, None, None], scores_again, -1e30) - log_total)
    grad_weights = jnp.einsum(
        "btgrd,bugd->bgrtu", grad_mixed, values_low, preferred_element_type=wide_type
    )
    grad_values = jnp.einsum(
        "bgrtu,btgrd->bugd",
        weights_again.astype(low_type),
        grad_mixed,
        preferred_element_type=wide_type,
    )
    grad_values = grad_values.astype(low_type).reshape(rows_all, kv_here * HEAD_DIM)
    row_delta = jnp.sum(weights_again * grad_weights, axis=-1, keepdims=True)
    grad_scores = (weights_again * (grad_weights - row_delta)).astype(low_type)
    grad_query_rot = (
        jnp.einsum("bgrtu,bugd->btgrd", grad_scores, keys_rot, preferred_element_type=wide_type)
        * score_scale
    )
    grad_keys_rot = (
        jnp.einsum("bgrtu,btgrd->bugd", grad_scores, query_rot, preferred_element_type=wide_type)
        * score_scale
    )
    grad_query = (
        rotate(grad_query_rot.reshape(blocks, block_rows, heads_here, HEAD_DIM), cosine, -sine_part)
        .astype(low_type)
        .reshape(rows_all, heads_here * HEAD_DIM)
    )
    grad_keys = (
        rotate(grad_keys_rot, cosine, -sine_part)
        .astype(low_type)
        .reshape(rows_all, kv_here * HEAD_DIM)
    )
    grad_w_query = jnp.einsum("tc,te->ce", normed, grad_query, preferred_element_type=wide_type)
    grad_w_key = jnp.einsum("tc,te->ce", normed, grad_keys, preferred_element_type=wide_type)
    grad_w_value = jnp.einsum("tc,te->ce", normed, grad_values, preferred_element_type=wide_type)
    grad_normed = jnp.einsum("te,ce->tc", grad_query, query_back, preferred_element_type=wide_type)
    grad_normed = grad_normed + jnp.einsum(
        "te,ce->tc", grad_keys, key_back, preferred_element_type=wide_type
    )
    grad_normed = grad_normed + jnp.einsum(
        "te,ce->tc", grad_values, value_back, preferred_element_type=wide_type
    )
    grad_gain_attn = jnp.sum(grad_normed * unit_attn, axis=0)
    scaled_attn = grad_normed * gain_one
    grad_inputs = grad_hidden + inv_first * (
        scaled_attn - unit_attn * jnp.mean(scaled_attn * unit_attn, axis=-1, keepdims=True)
    )
    grad_tokens = grad_inputs.astype(low_type)
    attn_grads = reduce_attention(
        grad_gain_attn, grad_w_query, grad_w_key, grad_w_value, grad_w_out
    )
    return (
        layer_out,
        grad_tokens,
        attn_grads[0],
        attn_grads[1],
        attn_grads[2],
        attn_grads[3],
        attn_grads[4],
        feed_grads[0],
        feed_grads[1],
        feed_grads[2],
        feed_grads[3],
    )


def solution(mesh):
    placed = (
        P(("dp", "fsdp"), None),
        P(("dp", "fsdp")),
        P("dp"),
        P("dp", "fsdp"),
        P("dp", "fsdp"),
        P("dp", "fsdp"),
        P("fsdp", "dp"),
        P("dp"),
        P("dp", "fsdp"),
        P("dp", "fsdp"),
        P("fsdp", "dp"),
        P(("dp", "fsdp"), None),
    )
    return jax.shard_map(
        on_device,
        mesh=mesh,
        in_specs=placed,
        out_specs=(
            P(("dp", "fsdp"), None),
            P(("dp", "fsdp"), None),
            P("dp"),
            P("dp", "fsdp"),
            P("dp", "fsdp"),
            P("dp", "fsdp"),
            P("fsdp", "dp"),
            P("dp"),
            P("dp", "fsdp"),
            P("dp", "fsdp"),
            P("fsdp", "dp"),
        ),
        check_vma=False,
    )
```

profile of v0, /device:TPU:0, one launch (start us, length us, event | category | flops | bytes accessed | tf_op | source)
XLA Modules:
  0.0 2389.2 jit_solution(8841014630282834477)
XLA Ops:
  14.7 35.2 %all_gather.65 = bf16[2048,64]{0,1:T(8,128)(2,1)} all-gather(bf16[256,64]{0,1:T(8,128)(2,1)S(1)} %convert_element_type.225), channel_id=1, replica_groups=mesh['dp'=8,'fsdp'=4] {'dp'}, dimensions={0}, use_global_device_ids=true | all-gather | bytes 294912 | tf_op jit(solution)/shard_map/all_gather | solution.py:44
  50.0 33.1 %all_gather.63 = bf16[2048,64]{0,1:T(8,128)(2,1)} all-gather(bf16[256,64]{0,1:T(8,128)(2,1)S(1)} %convert_element_type.223), channel_id=1, replica_groups=mesh['dp'=8,'fsdp'=4] {'dp'}, dimensions={0}, use_global_device_ids=true | all-gather | bytes 294912 | tf_op jit(solution)/shard_map/all_gather | solution.py:45
  84.0 34.4 %all-gather.23.cloned.1.call-done = bf16[512,2048]{1,0:T(8,128)(2,1)} async-done(((bf16[512,256]{1,0:T(8,128)(2,1)}), bf16[512,2048]{1,0:T(8,128)(2,1)}) %all-gather.23.cloned.1.call-update) | async-done | bytes 2097168 | tf_op jit(solution)/shard_map/all_gather | solution.py:46
  118.4 93.6 %all-gather.27.cloned.1.call-done = bf16[2048,1408]{1,0:T(8,128)(2,1)} async-done(((bf16[256,1408]{1,0:T(8,128)(2,1)}), bf16[2048,1408]{1,0:T(8,128)(2,1)}) %all-gather.27.cloned.1.call-update) | async-done | bytes 5767184 | tf_op jit(solution)/shard_map/all_gather | solution.py:61
  212.1 93.4 %all-gather.31.cloned.1.call-done = bf16[2048,1408]{1,0:T(8,128)(2,1)} async-done(((bf16[256,1408]{1,0:T(8,128)(2,1)}), bf16[2048,1408]{1,0:T(8,128)(2,1)}) %all-gather.31.cloned.1.call-update) | async-done | bytes 5767184 | tf_op jit(solution)/shard_map/all_gather | solution.py:62
  305.5 94.2 %all-gather.35.cloned.1.call-done = bf16[1408,2048]{1,0:T(8,128)(2,1)} async-done(((bf16[1408,256]{1,0:T(8,128)(2,1)}), bf16[1408,2048]{1,0:T(8,128)(2,1)}) %all-gather.35.cloned.1.call-update) | async-done | bytes 5767184 | tf_op jit(solution)/shard_map/all_gather | solution.py:63
  440.3 54.0 %all-gather.21.cloned.1.call-done = bf16[2048,2048]{1,0:T(8,128)(2,1)} async-done(((bf16[2048,512]{1,0:T(8,128)(2,1)}), bf16[2048,2048]{1,0:T(8,128)(2,1)}) %all-gather.21.cloned.1.call-update) | async-done | bytes 8388624 | tf_op jit(solution)/shard_map/all_gather | solution.py:49
  510.3 43.9 %all-gather.25.cloned.1.call-done = bf16[2048,2048]{1,0:T(8,128)(2,1)} async-done(((bf16[512,2048]{1,0:T(8,128)(2,1)}), bf16[2048,2048]{1,0:T(8,128)(2,1)}) %all-gather.25.cloned.1.call-update) | async-done | bytes 8388624 | tf_op jit(solution)/shard_map/all_gather | solution.py:52
  562.0 136.7 %all-gather.29.cloned.1.call-done = bf16[2048,5632]{1,0:T(8,128)(2,1)} async-done(((bf16[2048,1408]{1,0:T(8,128)(2,1)}), bf16[2048,5632]{1,0:T(8,128)(2,1)}) %all-gather.29.cloned.1.call-update) | async-done | bytes 23068688 | tf_op jit(solution)/shard_map/all_gather | solution.py:66
  711.8 131.7 %all-gather.33.cloned.1.call-done = bf16[2048,5632]{1,0:T(8,128)(2,1)} async-done(((bf16[2048,1408]{1,0:T(8,128)(2,1)}), bf16[2048,5632]{1,0:T(8,128)(2,1)}) %all-gather.33.cloned.1.call-update) | async-done | bytes 23068688 | tf_op jit(solution)/shard_map/all_gather | solution.py:67
  856.6 131.6 %all-gather.37.cloned.1.call-done = bf16[5632,2048]{1,0:T(8,128)(2,1)} async-done(((bf16[1408,2048]{1,0:T(8,128)(2,1)}), bf16[5632,2048]{1,0:T(8,128)(2,1)}) %all-gather.37.cloned.1.call-update) | async-done | bytes 23068688 | tf_op jit(solution)/shard_map/all_gather | solution.py:68
  1096.1 30.9 %copy.62 = bf16[2048,5632]{0,1:T(8,128)(2,1)} copy(bf16[2048,5632]{1,0:T(8,128)(2,1)} %convolution_convert_fusion.2) | data formatting | bytes 46137344
  1140.5 29.0 %copy.64 = bf16[2048,5632]{0,1:T(8,128)(2,1)} copy(bf16[2048,5632]{1,0:T(8,128)(2,1)} %convolution_convert_fusion.1) | data formatting | bytes 46137344
  1185.1 74.3 %reduce-scatter.31.cloned.1.call-done = bf16[512,2048]{1,0:T(8,128)(2,1)} async-done(((bf16[2048,2048]{1,0:T(8,128)(2,1)}), bf16[512,2048]{1,0:T(8,128)(2,1)}) %reduce-scatter.31.cloned.1.call-update) | async-done | bytes 2097168 | tf_op jit(solution)/shard_map/reduce_scatter | solution.py:90
  1259.4 169.2 %reduce-scatter.43.cloned.1.call-done = bf16[1408,2048]{1,0:T(8,128)(2,1)} async-done(((bf16[5632,2048]{1,0:T(8,128)(2,1)}), bf16[1408,2048]{1,0:T(8,128)(2,1)}) %reduce-scatter.43.cloned.1.call-update) | async-done | bytes 5767184
  1436.9 161.1 %reduce-scatter.45.cloned.1.call-done = bf16[1408,2048]{1,0:T(8,128)(2,1)} async-done(((bf16[5632,2048]{1,0:T(8,128)(2,1)}), bf16[1408,2048]{1,0:T(8,128)(2,1)}) %reduce-scatter.45.cloned.1.call-update) | async-done | bytes 5767184
  1606.5 160.9 %reduce-scatter.39.cloned.1.call-done = bf16[1408,2048]{1,0:T(8,128)(2,1)} async-done(((bf16[5632,2048]{1,0:T(8,128)(2,1)}), bf16[1408,2048]{1,0:T(8,128)(2,1)}) %reduce-scatter.39.cloned.1.call-update) | async-done | bytes 5767184 | tf_op jit(solution)/shard_map/reduce_scatter | solution.py:127
  1791.0 21.9 all-reduce.4
  1834.0 63.0 %reduce-scatter.29.cloned.1.call-done = bf16[256,64]{0,1:T(8,128)(2,1)} async-done(((bf16[2048,64]{0,1:T(8,128)(2,1)}), bf16[256,64]{0,1:T(8,128)(2,1)}) %reduce-scatter.29.cloned.1.call-update) | async-done | bytes 32784 | tf_op jit(solution)/shard_map/reduce_scatter | solution.py:104
  1898.4 69.3 %reduce-scatter.21.cloned.1.call-done = bf16[256,512]{1,0:T(8,128)(2,1)} async-done(((bf16[2048,512]{1,0:T(8,128)(2,1)}), bf16[256,512]{1,0:T(8,128)(2,1)}) %reduce-scatter.21.cloned.1.call-update) | async-done | bytes 262160 | tf_op jit(solution)/shard_map/reduce_scatter | solution.py:98
  1969.5 69.5 %reduce-scatter.33.cloned.1.call-done = bf16[512,256]{1,0:T(8,128)(2,1)} async-done(((bf16[512,2048]{1,0:T(8,128)(2,1)}), bf16[512,256]{1,0:T(8,128)(2,1)}) %reduce-scatter.33.cloned.1.call-update) | async-done | bytes 262160 | tf_op jit(solution)/shard_map/reduce_scatter | solution.py:107
  2040.8 111.1 %reduce-scatter.35.cloned.1.call-done = bf16[256,1408]{1,0:T(8,128)(2,1)} async-done(((bf16[2048,1408]{1,0:T(8,128)(2,1)}), bf16[256,1408]{1,0:T(8,128)(2,1)}) %reduce-scatter.35.cloned.1.call-update) | async-done | bytes 720912 | tf_op jit(solution)/shard_map/reduce_scatter | solution.py:135
  2154.2 111.6 %reduce-scatter.37.cloned.1.call-done = bf16[256,1408]{1,0:T(8,128)(2,1)} async-done(((bf16[2048,1408]{1,0:T(8,128)(2,1)}), bf16[256,1408]{1,0:T(8,128)(2,1)}) %reduce-scatter.37.cloned.1.call-update) | async-done | bytes 720912 | tf_op jit(solution)/shard_map/reduce_scatter | solution.py:138
  2268.1 111.9 %reduce-scatter.41.cloned.1.call-done = bf16[1408,256]{1,0:T(8,128)(2,1)} async-done(((bf16[1408,2048]{1,0:T(8,128)(2,1)}), bf16[1408,256]{1,0:T(8,128)(2,1)}) %reduce-scatter.41.cloned.1.call-update) | async-done | bytes 720912 | tf_op jit(solution)/shard_map/reduce_scatter | solution.py:141
  (209 shorter events, 307.3 us)
Async XLA Ops:
  11.0 200.9 %all-gather.27.cloned.1.call-start = ((), (), s32[]{:S(2)}) async-start(), calls=%async_computation.20 | async-start | bytes 6488064 | tf_op jit(solution)/shard_map/all_gather | solution.py:61
  12.1 293.4 %all-gather.31.cloned.1.call-start = ((), (), s32[]{:S(2)}) async-start(), calls=%async_computation.22 | async-start | bytes 6488064 | tf_op jit(solution)/shard_map/all_gather | solution.py:62
  13.1 386.6 %all-gather.35.cloned.1.call-start = ((), (), s32[]{:S(2)}) async-start(), calls=%async_computation.24 | async-start | bytes 6488064 | tf_op jit(solution)/shard_map/all_gather | solution.py:63
  14.6 422.0 %all-gather.17.cloned.1.call-start = ((), (), s32[]{:S(2)}) async-start(), calls=%async_computation.15 | async-start | bytes 1310720 | tf_op jit(solution)/shard_map/all_gather | solution.py:50
  49.9 388.5 %all-gather.15.cloned.1.call-start = ((), (), s32[]{:S(2)}) async-start(), calls=%async_computation.14 | async-start | bytes 1310720 | tf_op jit(solution)/shard_map/all_gather | solution.py:51
  83.2 411.2 %all-gather.21.cloned.1.call-start = ((), (), s32[]{:S(2)}) async-start(), calls=%async_computation.17 | async-start | bytes 10485760 | tf_op jit(solution)/shard_map/all_gather | solution.py:49
  83.9 470.3 %all-gather.25.cloned.1.call-start = ((), (), s32[]{:S(2)}) async-start(), calls=%async_computation.19 | async-start | bytes 10485760 | tf_op jit(solution)/shard_map/all_gather | solution.py:52
  118.4 580.4 %all-gather.29.cloned.1.call-start = ((), (), s32[]{:S(2)}) async-start(), calls=%async_computation.21 | async-start | bytes 28835840 | tf_op jit(solution)/shard_map/all_gather | solution.py:66
  212.0 631.5 %all-gather.33.cloned.1.call-start = ((), (), s32[]{:S(2)}) async-start(), calls=%async_computation.23 | async-start | bytes 28835840 | tf_op jit(solution)/shard_map/all_gather | solution.py:67
  305.5 682.7 %all-gather.37.cloned.1.call-start = ((), (), s32[]{:S(2)}) async-start(), calls=%async_computation.25 | async-start | bytes 28835840 | tf_op jit(solution)/shard_map/all_gather | solution.py:68
  399.8 782.4 %reduce-scatter.23.cloned.1.call-start = ((), (), s32[]{:S(2)}) async-start(), calls=%async_computation.28 | async-start | bytes 1310720 | tf_op jit(solution)/shard_map/reduce_scatter | solution.py:84
  1057.7 125.0 %reduce-scatter.27.cloned.1.call-start = ((), (), s32[]{:S(2)}) async-start(), calls=%async_computation.30 | async-start | bytes 1310720 | tf_op jit(solution)/shard_map/reduce_scatter | solution.py:87
  1064.5 120.5 %reduce-scatter.19.cloned.1.call-start = ((), (), s32[]{:S(2)}) async-start(), calls=%async_computation.26 | async-start | bytes 10485760 | tf_op jit(solution)/shard_map/reduce_scatter | solution.py:81
  1076.1 183.3 %reduce-scatter.31.cloned.1.call-start = ((), (), s32[]{:S(2)}) async-start(), calls=%async_computation.32 | async-start | bytes 10485760 | tf_op jit(solution)/shard_map/reduce_scatter | solution.py:90
  1083.0 345.6 %reduce-scatter.43.cloned.1.call-start = ((), (), s32[]{:S(2)}) async-start(), calls=%async_computation.38 | async-start | bytes 28835840
  1127.0 471.0 %reduce-scatter.45.cloned.1.call-start = ((), (), s32[]{:S(2)}) async-start(), calls=%async_computation.39 | async-start | bytes 28835840
  1169.4 598.0 %reduce-scatter.39.cloned.1.call-start = ((), (), s32[]{:S(2)}) async-start(), calls=%async_computation.36 | async-start | bytes 28835840 | tf_op jit(solution)/shard_map/reduce_scatter | solution.py:127
  1182.1 650.5 %reduce-scatter.25.cloned.1.call-start = ((), (), s32[]{:S(2)}) async-start(), calls=%async_computation.29 | async-start | bytes 294912 | tf_op jit(solution)/shard_map/reduce_scatter | solution.py:101
  1182.7 714.4 %reduce-scatter.29.cloned.1.call-start = ((), (), s32[]{:S(2)}) async-start(), calls=%async_computation.31 | async-start | bytes 294912 | tf_op jit(solution)/shard_map/reduce_scatter | solution.py:104
  1183.4 784.3 %reduce-scatter.21.cloned.1.call-start = ((), (), s32[]{:S(2)}) async-start(), calls=%async_computation.27 | async-start | bytes 2359296 | tf_op jit(solution)/shard_map/reduce_scatter | solution.py:98
  1185.0 854.0 %reduce-scatter.33.cloned.1.call-start = ((), (), s32[]{:S(2)}) async-start(), calls=%async_computation.33 | async-start | bytes 2359296 | tf_op jit(solution)/shard_map/reduce_scatter | solution.py:107
  1259.4 892.5 %reduce-scatter.35.cloned.1.call-start = ((), (), s32[]{:S(2)}) async-start(), calls=%async_computation.34 | async-start | bytes 6488064 | tf_op jit(solution)/shard_map/reduce_scatter | solution.py:135
  1436.9 828.9 %reduce-scatter.37.cloned.1.call-start = ((), (), s32[]{:S(2)}) async-start(), calls=%async_computation.35 | async-start | bytes 6488064 | tf_op jit(solution)/shard_map/reduce_scatter | solution.py:138
  1606.5 773.5 %reduce-scatter.41.cloned.1.call-start = ((), (), s32[]{:S(2)}) async-start(), calls=%async_computation.37 | async-start | bytes 6488064 | tf_op jit(solution)/shard_map/reduce_scatter | solution.py:141
  (31 other events, 1519.1 us)
Sparse Core Ops, SparseCore 0:
  10.7 55.1 all-gather.18
  68.6 49.7 all-gather.22
  121.1 90.8 all-gather.26
  214.6 90.8 all-gather.30
  307.9 91.7 all-gather.34
  436.0 58.2 all-gather.20
  495.9 58.2 all-gather.24
  555.6 143.1 all-gather.28
  700.4 143.1 all-gather.32
  844.9 143.2 all-gather.36
  1057.9 24.8 reduce-scatter.22
  1085.9 24.8 reduce-scatter.26
  1113.2 71.7 reduce-scatter.18
  1187.6 71.6 reduce-scatter.30
  1261.8 166.7 reduce-scatter.42
  1431.2 166.7 reduce-scatter.44
  1600.6 166.7 reduce-scatter.38
  1771.0 61.6 reduce-scatter.24
  1836.3 60.6 reduce-scatter.28
  1901.0 66.6 reduce-scatter.20
  1971.7 67.2 reduce-scatter.32
  2043.0 108.9 reduce-scatter.34
  2156.0 109.7 reduce-scatter.36
  2269.8 110.1 reduce-scatter.40
  (2 shorter events, 31.5 us)
where the time goes:
time: 2400 us; the launch traced here: 2390 us
  waiting for transfers between devices  1920 us (80%)
  matrix products  189 us (8%)
  blocking collectives  135 us (6%)
  local copies, waits for them, and re-layouts  88.9 us (4%)
  other arithmetic  35.7 us (1%)
    unnamed x28, waiting for transfers between devices  333 us
    reduce_scatter x1, waiting for transfers between devices, reduce_feed(): lax.psum_scatter(grad_down.astype(jnp.bfloat16), 'fsdp', scatter_dimensio...  161 us
    all_gather x1, waiting for transfers between devices, feed_weights(): lax.all_gather(rows_full[1], 'fsdp', axis=1, tiled=True)  137 us
    all_gather x1, waiting for transfers between devices, feed_weights(): lax.all_gather(rows_full[2], 'fsdp', axis=1, tiled=True)  132 us
    all_gather x1, waiting for transfers between devices, feed_weights(): lax.all_gather(rows_full[3], 'fsdp', axis=0, tiled=True)  132 us
    reduce_scatter x1, waiting for transfers between devices, reduce_feed(): lax.psum_scatter(terms[3].astype(jnp.bfloat16), 'dp', scatter_dimension=1...  112 us
    reduce_scatter x1, waiting for transfers between devices, reduce_feed(): lax.psum_scatter(terms[2].astype(jnp.bfloat16), 'dp', scatter_dimension=0...  112 us
    reduce_scatter x1, waiting for transfers between devices, reduce_feed(): lax.psum_scatter(terms[1].astype(jnp.bfloat16), 'dp', scatter_dimension=0...  111 us
  transfers between devices with their start and end apart: 26, of which 21 were waited for; matrix products, arithmetic and copies ran while one was open for 10% of the time, Pallas kernels for 0%

commit v1 on v0

--- a/solution.py
+++ b/solution.py
@@ -7,6 +7,28 @@
 HEAD_DIM = 64
 EPSILON = 1e-05
 rope_base = 10000.0
+
+
+def joined_along(parts, dim):
+    lengths = list(parts.shape[1:])
+    lengths[dim] *= parts.shape[0]
+    return jnp.moveaxis(parts, 0, dim).reshape(lengths)
+
+
+def collected_by_bits(x, axis):
+    size = lax.axis_size(axis)
+    tiles = x[None]
+    for level in range(size.bit_length() - 1):
+        bit = 1 << level
+        partner_block = lax.ppermute(tiles, axis, [(i, i ^ bit) for i in range(size)])
+        both = jnp.stack([tiles, partner_block])
+        upper = lax.axis_index(axis) >> level & 1
+        tiles = jnp.where(upper == 0, both, both[::-1]).reshape(-1, *x.shape)
+    return tiles
+
+
+def collect(array, axis, dim):
+    return joined_along(collected_by_bits(array, axis), dim)
 
 
 def tables(segment_block):
@@ -60,7 +82,7 @@
         lax.all_gather(gain_mlp.astype(low_type), "dp", axis=0, tiled=True),
         lax.all_gather(w_gate.astype(low_type), "dp", axis=0, tiled=True),
         lax.all_gather(w_up.astype(low_type), "dp", axis=0, tiled=True),
-        lax.all_gather(w_down.astype(low_type), "dp", axis=1, tiled=True),
+        collect(w_down.astype(low_type), "dp", 1),
     )
     wide_cols = (
         lax.all_gather(rows_full[1], "fsdp", axis=1, tiled=True),

time: 2400 us -> 2300 us (0.958)
  waiting for transfers between devices: 1920 us -> 1810 us
    ppermute x0 -> x3, waiting for transfers between devices: none -> 168 us  [collected_by_bits(): lax.ppermute(tiles, axis, [(i, i ^ bit) for i in range(size)])]
    all_gather x1 -> x0, waiting for transfers between devices: 94.2 us -> none  [feed_weights(): lax.all_gather(w_down.astype(low_type), 'dp', axis=1, tiled=True)]
    all_gather x1, waiting for transfers between devices: 137 us -> 46.2 us  [feed_weights(): lax.all_gather(rows_full[1], 'fsdp', axis=1, tiled=True)]
    all_gather x1, waiting for transfers between devices: 54 us -> 0.02 us  [attention_weights(): lax.all_gather(rows_full[1], 'fsdp', axis=1, tiled=True)]
    all_gather x1, waiting for transfers between devices: 43.9 us -> 0.01 us  [attention_weights(): lax.all_gather(rows_full[4], 'fsdp', axis=0, tiled=True)]
    unnamed x72 -> x68, local copies, waits for them, and re-layouts: 86.6 us -> 86.2 us
    unnamed x28 -> x27, waiting for transfers between devices: 333 us -> 333 us
  transfers between devices with their start and end apart: 26 -> 28, of which waited for: 21 -> 21; matrix products, arithmetic and copies ran while one was open for 10% -> 11% of each run, Pallas kernels for 0% -> 0%
where the time goes in v1:
time: 2300 us; the launch traced here: 2290 us
  waiting for transfers between devices  1810 us (79%)
  matrix products  188 us (8%)
  blocking collectives  138 us (6%)
  local copies, waits for them, and re-layouts  94 us (4%)
  other arithmetic  44.2 us (2%)
    unnamed x27, waiting for transfers between devices  333 us
    ppermute x3, waiting for transfers between devices, collected_by_bits(): lax.ppermute(tiles, axis, [(i, i ^ bit) for i in range(size)])  168 us
    reduce_scatter x1, waiting for transfers between devices, reduce_feed(): lax.psum_scatter(grad_down.astype(jnp.bfloat16), 'fsdp', scatter_dimensio...  161 us
    all_gather x1, waiting for transfers between devices, feed_weights(): lax.all_gather(rows_full[3], 'fsdp', axis=0, tiled=True)  132 us
    all_gather x1, waiting for transfers between devices, feed_weights(): lax.all_gather(rows_full[2], 'fsdp', axis=1, tiled=True)  131 us
    reduce_scatter x1, waiting for transfers between devices, reduce_feed(): lax.psum_scatter(terms[3].astype(jnp.bfloat16), 'dp', scatter_dimension=1...  112 us
    reduce_scatter x1, waiting for transfers between devices, reduce_feed(): lax.psum_scatter(terms[2].astype(jnp.bfloat16), 'dp', scatter_dimension=0...  111 us
    reduce_scatter x1, waiting for transfers between devices, reduce_feed(): lax.psum_scatter(terms[1].astype(jnp.bfloat16), 'dp', scatter_dimension=0...  111 us
  transfers between devices with their start and end apart: 28, of which 21 were waited for; matrix products, arithmetic and copies ran while one was open for 11% of the time, Pallas kernels for 0%

profile of v1, /device:TPU:0, one launch (start us, length us, event | category | flops | bytes accessed | tf_op | source)
XLA Modules:
  0.0 2292.9 jit_solution(6098093577211236838)
XLA Ops:
  13.2 35.4 %all_gather.61 = bf16[2048,64]{0,1:T(8,128)(2,1)} all-gather(bf16[256,64]{0,1:T(8,128)(2,1)S(1)} %convert_element_type.225), channel_id=1, replica_groups=mesh['dp'=8,'fsdp'=4] {'dp'}, dimensions={0}, use_global_device_ids=true | all-gather | bytes 294912 | tf_op jit(solution)/shard_map/all_gather | solution.py:66
  48.7 33.3 %all_gather.59 = bf16[2048,64]{0,1:T(8,128)(2,1)} all-gather(bf16[256,64]{0,1:T(8,128)(2,1)S(1)} %convert_element_type.223), channel_id=1, replica_groups=mesh['dp'=8,'fsdp'=4] {'dp'}, dimensions={0}, use_global_device_ids=true | all-gather | bytes 294912 | tf_op jit(solution)/shard_map/all_gather | solution.py:67
  82.8 35.5 %all-gather.22.cloned.1.call-done = bf16[512,2048]{1,0:T(8,128)(2,1)} async-done(((bf16[512,256]{1,0:T(8,128)(2,1)}), bf16[512,2048]{1,0:T(8,128)(2,1)}) %all-gather.22.cloned.1.call-update) | async-done | bytes 2097168 | tf_op jit(solution)/shard_map/all_gather | solution.py:68
  118.4 93.6 %all-gather.26.cloned.1.call-done = bf16[2048,1408]{1,0:T(8,128)(2,1)} async-done(((bf16[256,1408]{1,0:T(8,128)(2,1)}), bf16[2048,1408]{1,0:T(8,128)(2,1)}) %all-gather.26.cloned.1.call-update) | async-done | bytes 5767184 | tf_op jit(solution)/shard_map/all_gather | solution.py:83
  212.0 93.4 %all-gather.30.cloned.1.call-done = bf16[2048,1408]{1,0:T(8,128)(2,1)} async-done(((bf16[256,1408]{1,0:T(8,128)(2,1)}), bf16[2048,1408]{1,0:T(8,128)(2,1)}) %all-gather.30.cloned.1.call-update) | async-done | bytes 5767184 | tf_op jit(solution)/shard_map/all_gather | solution.py:84
  324.7 31.8 %collective-permute-done.1 = bf16[2,1408,256]{2,1,0:T(8,128)(2,1)} collective-permute-done((bf16[2,1408,256]{2,1,0:T(8,128)(2,1)S(1)}, bf16[2,1408,256]{2,1,0:T(8,128)(2,1)}, u32[]{:S(2)}, u32[]{:S(2)}) %collective-permute-start.1) | collective-permute-done | bytes 1441824 | tf_op jit(solution)/shard_map/ppermute | solution.py:23
  366.3 120.0 %collective-permute-done.2 = bf16[4,1408,256]{1,2,0:T(8,128)(2,1)} collective-permute-done((bf16[4,1408,256]{1,2,0:T(8,128)(2,1)}, bf16[4,1408,256]{1,2,0:T(8,128)(2,1)}, u32[]{:S(2)}, u32[]{:S(2)}) %collective-permute-start.2) | collective-permute-done | bytes 2883616 | tf_op jit(solution)/shard_map/ppermute | solution.py:23
  493.9 19.7 all-gather
  558.3 46.2 %all-gather.28.cloned.1.call-done = bf16[2048,5632]{1,0:T(8,128)(2,1)} async-done(((bf16[2048,1408]{1,0:T(8,128)(2,1)}), bf16[2048,5632]{1,0:T(8,128)(2,1)}) %all-gather.28.cloned.1.call-update) | async-done | bytes 23068688 | tf_op jit(solution)/shard_map/all_gather | solution.py:88
  617.6 131.4 %all-gather.32.cloned.1.call-done = bf16[2048,5632]{1,0:T(8,128)(2,1)} async-done(((bf16[2048,1408]{1,0:T(8,128)(2,1)}), bf16[2048,5632]{1,0:T(8,128)(2,1)}) %all-gather.32.cloned.1.call-update) | async-done | bytes 23068688 | tf_op jit(solution)/shard_map/all_gather | solution.py:89
  762.1 131.7 %all-gather.34.cloned.1.call-done = bf16[5632,2048]{0,1:T(8,128)(2,1)} async-done(((bf16[1408,2048]{0,1:T(8,128)(2,1)}), bf16[5632,2048]{0,1:T(8,128)(2,1)}) %all-gather.34.cloned.1.call-update) | async-done | bytes 23068688 | tf_op jit(solution)/shard_map/all_gather | solution.py:90
  999.9 30.8 %copy.73 = bf16[2048,5632]{0,1:T(8,128)(2,1)} copy(bf16[2048,5632]{1,0:T(8,128)(2,1)} %convolution_convert_fusion.2) | data formatting | bytes 46137344
  1044.4 28.9 %copy.75 = bf16[2048,5632]{0,1:T(8,128)(2,1)} copy(bf16[2048,5632]{1,0:T(8,128)(2,1)} %convolution_convert_fusion.1) | data formatting | bytes 46137344
  1089.0 74.3 %reduce-scatter.31.cloned.1.call-done = bf16[512,2048]{1,0:T(8,128)(2,1)} async-done(((bf16[2048,2048]{1,0:T(8,128)(2,1)}), bf16[512,2048]{1,0:T(8,128)(2,1)}) %reduce-scatter.31.cloned.1.call-update) | async-done | bytes 2097168 | tf_op jit(solution)/shard_map/reduce_scatter | solution.py:112
  1163.4 169.2 %reduce-scatter.43.cloned.1.call-done = bf16[1408,2048]{1,0:T(8,128)(2,1)} async-done(((bf16[5632,2048]{1,0:T(8,128)(2,1)}), bf16[1408,2048]{1,0:T(8,128)(2,1)}) %reduce-scatter.43.cloned.1.call-update) | async-done | bytes 5767184
  1340.9 161.1 %reduce-scatter.45.cloned.1.call-done = bf16[1408,2048]{1,0:T(8,128)(2,1)} async-done(((bf16[5632,2048]{1,0:T(8,128)(2,1)}), bf16[1408,2048]{1,0:T(8,128)(2,1)}) %reduce-scatter.45.cloned.1.call-update) | async-done | bytes 5767184
  1510.4 160.8 %reduce-scatter.39.cloned.1.call-done = bf16[1408,2048]{1,0:T(8,128)(2,1)} async-done(((bf16[5632,2048]{1,0:T(8,128)(2,1)}), bf16[1408,2048]{1,0:T(8,128)(2,1)}) %reduce-scatter.39.cloned.1.call-update) | async-done | bytes 5767184 | tf_op jit(solution)/shard_map/reduce_scatter | solution.py:149
  1694.8 21.8 all-reduce.4
  1738.0 62.9 %reduce-scatter.29.cloned.1.call-done = bf16[256,64]{0,1:T(8,128)(2,1)} async-done(((bf16[2048,64]{0,1:T(8,128)(2,1)}), bf16[256,64]{0,1:T(8,128)(2,1)}) %reduce-scatter.29.cloned.1.call-update) | async-done | bytes 32784 | tf_op jit(solution)/shard_map/reduce_scatter | solution.py:126
  1802.3 69.2 %reduce-scatter.21.cloned.1.call-done = bf16[256,512]{1,0:T(8,128)(2,1)} async-done(((bf16[2048,512]{1,0:T(8,128)(2,1)}), bf16[256,512]{1,0:T(8,128)(2,1)}) %reduce-scatter.21.cloned.1.call-update) | async-done | bytes 262160 | tf_op jit(solution)/shard_map/reduce_scatter | solution.py:120
  1873.3 69.3 %reduce-scatter.33.cloned.1.call-done = bf16[512,256]{1,0:T(8,128)(2,1)} async-done(((bf16[512,2048]{1,0:T(8,128)(2,1)}), bf16[512,256]{1,0:T(8,128)(2,1)}) %reduce-scatter.33.cloned.1.call-update) | async-done | bytes 262160 | tf_op jit(solution)/shard_map/reduce_scatter | solution.py:129
  1944.4 111.3 %reduce-scatter.35.cloned.1.call-done = bf16[256,1408]{1,0:T(8,128)(2,1)} async-done(((bf16[2048,1408]{1,0:T(8,128)(2,1)}), bf16[256,1408]{1,0:T(8,128)(2,1)}) %reduce-scatter.35.cloned.1.call-update) | async-done | bytes 720912 | tf_op jit(solution)/shard_map/reduce_scatter | solution.py:157
  2058.1 111.5 %reduce-scatter.37.cloned.1.call-done = bf16[256,1408]{1,0:T(8,128)(2,1)} async-done(((bf16[2048,1408]{1,0:T(8,128)(2,1)}), bf16[256,1408]{1,0:T(8,128)(2,1)}) %reduce-scatter.37.cloned.1.call-update) | async-done | bytes 720912 | tf_op jit(solution)/shard_map/reduce_scatter | solution.py:160
  2171.8 112.0 %reduce-scatter.41.cloned.1.call-done = bf16[1408,256]{1,0:T(8,128)(2,1)} async-done(((bf16[1408,2048]{1,0:T(8,128)(2,1)}), bf16[1408,256]{1,0:T(8,128)(2,1)}) %reduce-scatter.41.cloned.1.call-update) | async-done | bytes 720912 | tf_op jit(solution)/shard_map/reduce_scatter | solution.py:163
  (216 shorter events, 321.3 us)
Async XLA Ops:
  11.1 200.9 %all-gather.26.cloned.1.call-start = ((), (), s32[]{:S(2)}) async-start(), calls=%async_computation.20 | async-start | bytes 6488064 | tf_op jit(solution)/shard_map/all_gather | solution.py:83
  12.1 293.3 %all-gather.30.cloned.1.call-start = ((), (), s32[]{:S(2)}) async-start(), calls=%async_computation.22 | async-start | bytes 6488064 | tf_op jit(solution)/shard_map/all_gather | solution.py:84
  13.1 518.6 %all-gather.16.cloned.1.call-start = ((), (), s32[]{:S(2)}) async-start(), calls=%async_computation.15 | async-start | bytes 1310720 | tf_op jit(solution)/shard_map/all_gather | solution.py:72
  48.6 485.1 %all-gather.14.cloned.1.call-start = ((), (), s32[]{:S(2)}) async-start(), calls=%async_computation.14 | async-start | bytes 1310720 | tf_op jit(solution)/shard_map/all_gather | solution.py:73
  82.0 453.5 %all-gather.20.cloned.1.call-start = ((), (), s32[]{:S(2)}) async-start(), calls=%async_computation.17 | async-start | bytes 10485760 | tf_op jit(solution)/shard_map/all_gather | solution.py:71
  82.8 467.6 %all-gather.24.cloned.1.call-start = ((), (), s32[]{:S(2)}) async-start(), calls=%async_computation.19 | async-start | bytes 10485760 | tf_op jit(solution)/shard_map/all_gather | solution.py:74
  118.4 486.1 %all-gather.28.cloned.1.call-start = ((), (), s32[]{:S(2)}) async-start(), calls=%async_computation.21 | async-start | bytes 28835840 | tf_op jit(solution)/shard_map/all_gather | solution.py:88
  212.0 537.0 %all-gather.32.cloned.1.call-start = ((), (), s32[]{:S(2)}) async-start(), calls=%async_computation.23 | async-start | bytes 28835840 | tf_op jit(solution)/shard_map/all_gather | solution.py:89
  305.5 588.3 %all-gather.34.cloned.1.call-start = ((), (), s32[]{:S(2)}) async-start(), calls=%async_computation.24 | async-start | bytes 28835840 | tf_op jit(solution)/shard_map/all_gather | solution.py:90
  361.5 124.8 %collective-permute-start.2 = (bf16[4,1408,256]{1,2,0:T(8,128)(2,1)}, bf16[4,1408,256]{1,2,0:T(8,128)(2,1)}, u32[]{:S(2)}, u32[]{:S(2)}) collective-permute-start(bf16[4,1408,256]{1,2,0:T(8,128)(2,1)} %copy.56), channel_id=1, source_target_pairs={{0,16},{4,20},{8,24},{12,28},{16,0},{20,4},{24,8},{28,12},{1,17},{... | collective-permute-start | bytes 8650760 | tf_op jit(solution)/shard_map/ppermute | solution.py:23
  493.2 592.9 %reduce-scatter.23.cloned.1.call-start = ((), (), s32[]{:S(2)}) async-start(), calls=%async_computation.27 | async-start | bytes 1310720 | tf_op jit(solution)/shard_map/reduce_scatter | solution.py:106
  961.6 125.3 %reduce-scatter.27.cloned.1.call-start = ((), (), s32[]{:S(2)}) async-start(), calls=%async_computation.29 | async-start | bytes 1310720 | tf_op jit(solution)/shard_map/reduce_scatter | solution.py:109
  968.3 120.7 %reduce-scatter.19.cloned.1.call-start = ((), (), s32[]{:S(2)}) async-start(), calls=%async_computation.25 | async-start | bytes 10485760 | tf_op jit(solution)/shard_map/reduce_scatter | solution.py:103
  980.0 183.4 %reduce-scatter.31.cloned.1.call-start = ((), (), s32[]{:S(2)}) async-start(), calls=%async_computation.31 | async-start | bytes 10485760 | tf_op jit(solution)/shard_map/reduce_scatter | solution.py:112
  986.9 345.7 %reduce-scatter.43.cloned.1.call-start = ((), (), s32[]{:S(2)}) async-start(), calls=%async_computation.37 | async-start | bytes 28835840
  1030.8 471.2 %reduce-scatter.45.cloned.1.call-start = ((), (), s32[]{:S(2)}) async-start(), calls=%async_computation.38 | async-start | bytes 28835840
  1073.4 597.9 %reduce-scatter.39.cloned.1.call-start = ((), (), s32[]{:S(2)}) async-start(), calls=%async_computation.35 | async-start | bytes 28835840 | tf_op jit(solution)/shard_map/reduce_scatter | solution.py:149
  1086.1 650.6 %reduce-scatter.25.cloned.1.call-start = ((), (), s32[]{:S(2)}) async-start(), calls=%async_computation.28 | async-start | bytes 294912 | tf_op jit(solution)/shard_map/reduce_scatter | solution.py:123
  1086.8 714.1 %reduce-scatter.29.cloned.1.call-start = ((), (), s32[]{:S(2)}) async-start(), calls=%async_computation.30 | async-start | bytes 294912 | tf_op jit(solution)/shard_map/reduce_scatter | solution.py:126
  1087.4 784.1 %reduce-scatter.21.cloned.1.call-start = ((), (), s32[]{:S(2)}) async-start(), calls=%async_computation.26 | async-start | bytes 2359296 | tf_op jit(solution)/shard_map/reduce_scatter | solution.py:120
  1089.0 853.7 %reduce-scatter.33.cloned.1.call-start = ((), (), s32[]{:S(2)}) async-start(), calls=%async_computation.32 | async-start | bytes 2359296 | tf_op jit(solution)/shard_map/reduce_scatter | solution.py:129
  1163.3 892.4 %reduce-scatter.35.cloned.1.call-start = ((), (), s32[]{:S(2)}) async-start(), calls=%async_computation.33 | async-start | bytes 6488064 | tf_op jit(solution)/shard_map/reduce_scatter | solution.py:157
  1340.8 828.7 %reduce-scatter.37.cloned.1.call-start = ((), (), s32[]{:S(2)}) async-start(), calls=%async_computation.34 | async-start | bytes 6488064 | tf_op jit(solution)/shard_map/reduce_scatter | solution.py:160
  1510.4 773.4 %reduce-scatter.41.cloned.1.call-start = ((), (), s32[]{:S(2)}) async-start(), calls=%async_computation.36 | async-start | bytes 6488064 | tf_op jit(solution)/shard_map/reduce_scatter | solution.py:163
  (31 other events, 1226.3 us)
Sparse Core Ops, SparseCore 0:
  10.7 54.9 all-gather.17
  68.3 49.9 all-gather.21
  121.1 90.8 all-gather.25
  214.6 90.8 all-gather.29
  323.2 16.7 all-gather.13
  341.5 58.2 all-gather.19
  401.4 58.2 all-gather.23
  461.3 143.1 all-gather.27
  605.9 143.1 all-gather.31
  750.6 143.1 all-gather.33
  961.7 24.8 reduce-scatter.22
  989.9 24.8 reduce-scatter.26
  1017.2 71.7 reduce-scatter.18
  1091.6 71.6 reduce-scatter.30
  1165.8 166.7 reduce-scatter.42
  1335.2 166.7 reduce-scatter.44
  1504.4 166.7 reduce-scatter.38
  1674.9 61.6 reduce-scatter.24
  1740.2 60.6 reduce-scatter.28
  1804.8 66.6 reduce-scatter.20
  1875.5 67.1 reduce-scatter.32
  1946.8 108.9 reduce-scatter.34
  2059.7 109.7 reduce-scatter.36
  2173.6 110.1 reduce-scatter.40
  (1 shorter events, 14.9 us)
